TPU v7x, 32 devices: a whole 2x2x4 slice. The times are simulated.
32 devices in a mesh: dp: 16 (over z, y, x), ctx: 2 (over core).
Axes of the slice: x: 2, y: 2, z: 4, core: 2. Of those that a mesh axis runs over, the one named last changes fastest.
Arguments:
- layer_in: bfloat16 [16, 256, 4096], P('dp', 'ctx'), may hold values from -6 to 6
- inner_act: bfloat16 [16, 256, 2176], P('dp', 'ctx'), may hold values from -6 to 6
- readout: bfloat16 [16, 256, 64], P('dp', 'ctx'), may hold values from -0.75 to 0.75
- w_in: bfloat16 [4096, 132], P('dp'), may hold values from -0.09375 to 0.09375
- a_log: float32 [68], replicated, may hold values from -3.9 to -1.6
- dt_bias: float32 [68], replicated, may hold values from -4 to -1
- d_skip: float32 [68], replicated, may hold values from 0.5 to 1.5
- grad_out: bfloat16 [16, 256, 2176], P('dp', 'ctx'), may hold values from -6 to 6
Outputs:
- grad_x: bfloat16 [16, 256, 2176], P('dp', 'ctx')
- grad_c: bfloat16 [16, 256, 64], P('dp', 'ctx')
- grad_proj: bfloat16 [16, 256, 132], P('dp', 'ctx')
- grad_w: float32 [4096, 132], P('dp', 'ctx')
All inputs are finite; a program needn't handle non-finite values.
Results may differ from a plain program's by a relative error of at most 0.015.
Values may be sent and summed in bfloat16 or wider, within the bound.
A program may use at most 64 MiB of HBM per device.

v0:
```python
import jax
import jax.numpy as jnp
from jax import lax
from jax.sharding import PartitionSpec as P

STATE = 64
BLOCK = 128


def entering(array, axis, join, neutral, backward):
    count = lax.axis_size(axis)
    place = lax.axis_index(axis)
    ahead = count - 1 - place if backward else place
    gathered = jax.tree.map(
        lambda a, kind: lax.all_gather(a.astype(kind), axis), array, (jnp.bfloat16, jnp.bfloat16)
    )
    state = jax.tree.map(lambda a, e: jnp.zeros_like(a) + jnp.asarray(e, a.dtype), array, neutral)

    def one(turn, state):
        source = count - 1 - turn if backward else turn
        return join(
            state,
            jax.tree.map(
                lambda a, own: lax.dynamic_index_in_dim(a, source, 0, False).astype(own.dtype),
                gathered,
                array,
            ),
        )

    return lax.fori_loop(0, ahead, one, state)


def prepare(projected, a_log, dt_bias):
    b_rows = projected[:, :STATE].astype(jnp.bfloat16)
    step_size = jax.nn.softplus(projected[:, STATE:] + dt_bias)
    decay_rate = -jnp.exp(a_log) * step_size
    return (b_rows, step_size, decay_rate)


def blocked(values, width):
    return values.reshape(values.shape[0] // BLOCK, BLOCK, width)


def split_blocks(projected, inner_rows, a_log, dt_bias):
    row_count = projected.shape[0]
    head_count = a_log.shape[0]
    head_width = inner_rows.shape[1] // head_count
    b_rows, step_size, decay_rate = prepare(projected, a_log, dt_bias)
    inner_blocks = inner_rows.reshape(row_count // BLOCK, BLOCK, head_count, head_width)
    step_blocks = jnp.swapaxes(blocked(step_size, head_count), 1, 2)
    cum_blocks = jnp.cumsum(jnp.swapaxes(blocked(decay_rate, head_count), 1, 2), axis=2)
    return (inner_blocks, blocked(b_rows, STATE), step_blocks, cum_blocks, decay_rate)


def state_input(inner_c, b_c, step_c, cum_c):
    to_end = jnp.exp(cum_c[:, -1:] - cum_c) * step_c
    weighted = (b_c.astype(jnp.float32)[None] * to_end[:, :, None]).astype(jnp.bfloat16)
    return jnp.einsum("shp,hsn->hpn", inner_c, weighted, preferred_element_type=jnp.float32)


def block_forward(projected, inner_rows, c_rows, a_log, dt_bias, d_skip, entry_state):
    row_count = projected.shape[0]
    inner_blocks, b_blocks, step_blocks, cum_blocks, decay_rate = split_blocks(
        projected, inner_rows, a_log, dt_bias
    )
    c_blocks = blocked(c_rows, STATE)
    position = jnp.arange(BLOCK)
    causal = position[:, None] >= position[None, :]

    def block_advance(carried, pieces):
        inner_c, b_c, c_c, step_c, cum_c = pieces
        scores = jnp.dot(c_c, b_c.T, preferred_element_type=jnp.float32)
        spread = cum_c[:, :, None] - cum_c[:, None, :]
        factor = jnp.where(causal, jnp.exp(jnp.where(causal, spread, 0.0)), 0.0)
        mixing = (scores[None] * factor * step_c[:, None, :]).astype(jnp.bfloat16)
        within = jnp.einsum("hts,shp->thp", mixing, inner_c, preferred_element_type=jnp.float32)
        added = state_input(inner_c, b_c, step_c, cum_c)
        carried_in = jnp.einsum(
            "tn,hpn->thp", c_c.astype(jnp.float32), carried, precision=lax.Precision.HIGHEST
        )
        carried_in = carried_in * jnp.exp(cum_c).T[:, :, None]
        result = (within + carried_in + d_skip[None, :, None] * inner_c.astype(jnp.float32)).astype(
            jnp.bfloat16
        )
        carried = jnp.exp(cum_c[:, -1])[:, None, None] * carried + added
        return (carried, result)

    final_state, outputs = lax.scan(
        block_advance, entry_state, (inner_blocks, b_blocks, c_blocks, step_blocks, cum_blocks)
    )
    return (outputs.reshape(row_count, inner_rows.shape[1]), final_state)


def local_summary(projected, inner_rows, a_log, dt_bias):
    inner_blocks, b_blocks, step_blocks, cum_blocks, decay_rate = split_blocks(
        projected, inner_rows, a_log, dt_bias
    )
    head_count = a_log.shape[0]
    head_width = inner_rows.shape[1] // head_count

    def local_advance(carried, pieces):
        inner_c, b_c, step_c, cum_c = pieces
        added = state_input(inner_c, b_c, step_c, cum_c)
        return (jnp.exp(cum_c[:, -1])[:, None, None] * carried + added, None)

    zero_state = jnp.zeros((head_count, head_width, STATE), jnp.float32)
    final_state, unused = lax.scan(
        local_advance, zero_state, (inner_blocks, b_blocks, step_blocks, cum_blocks)
    )
    return (jnp.exp(jnp.sum(decay_rate, axis=0)), final_state)


def entry_weights(projected, c_rows, grad_rows, a_log, dt_bias):
    b_rows, step_size, decay_rate = prepare(projected, a_log, dt_bias)
    row_count = projected.shape[0]
    head_count = a_log.shape[0]
    head_width = grad_rows.shape[1] // head_count
    growth = jnp.exp(jnp.cumsum(decay_rate, axis=0))
    weighted = (c_rows.astype(jnp.float32)[:, None, :] * growth[:, :, None]).astype(jnp.bfloat16)
    return jnp.einsum(
        "thp,thn->hpn",
        grad_rows.reshape(row_count, head_count, head_width),
        weighted,
        preferred_element_type=jnp.float32,
    )


def combine_carry(earlier, later):
    return (earlier[0] * later[0], later[1] + later[0][:, None, None] * earlier[1])


def pass_along(decay_total, summary, backward):
    identity = (jnp.ones_like(decay_total), jnp.zeros_like(summary))
    return entering((decay_total, summary), "ctx", combine_carry, identity, backward)


def per_device(layer_in, inner_act, readout, w_in, a_log, dt_bias, d_skip, grad_out):
    tokens = layer_in[0]
    inner_rows = inner_act[0]
    c_rows = readout[0]
    grad_rows = grad_out[0]
    w_full = lax.all_gather(w_in, "dp", axis=0, tiled=True)
    projected = jnp.dot(tokens, w_full, preferred_element_type=jnp.float32)
    decay_total, own_state = local_summary(projected, inner_rows, a_log, dt_bias)
    entry_part = entry_weights(projected, c_rows, grad_rows, a_log, dt_bias)
    entry_state = pass_along(decay_total, own_state, False)[1]
    exit_grad = pass_along(decay_total, entry_part, True)[1]

    def recompute(proj_val, inner_val, c_val):
        return block_forward(proj_val, inner_val, c_val, a_log, dt_bias, d_skip, entry_state)

    primal, pullback = jax.vjp(recompute, projected, inner_rows, c_rows)
    grad_p, grad_v, grad_r = pullback((grad_rows, exit_grad))
    proj_grad = grad_p.astype(jnp.bfloat16)
    seq_count = lax.axis_size("dp")
    contract = (((0,), (0,)), ((), ()))
    summed = lax.psum_scatter(
        lax.dot_general(tokens, proj_grad, contract, preferred_element_type=jnp.float32),
        "dp",
        scatter_dimension=0,
        tiled=True,
    )
    weight_grad = lax.psum_scatter(summed, "ctx", scatter_dimension=1, tiled=True)
    return (grad_v[None], grad_r[None], proj_grad[None], weight_grad / seq_count)


def solution(mesh):
    in_specs = (
        P("dp", "ctx", None),
        P("dp", "ctx", None),
        P("dp", "ctx", None),
        P("dp", None),
        P(),
        P(),
        P(),
        P("dp", "ctx", None),
    )
    out_specs = (P("dp", "ctx", None), P("dp", "ctx", None), P("dp", "ctx", None), P("dp", "ctx"))
    return jax.shard_map(
        per_device, mesh=mesh, in_specs=in_specs, out_specs=out_specs, check_vma=False
    )
```

profile of v0, /device:TPU:0, one launch (start us, length us, event | category | flops | bytes accessed | tf_op | source)
XLA Modules:
  0.0 213.8 jit_solution(7782846302152594224)
XLA Ops:
  7.2 0.7 all-gather.5.cloned.1.call-update
  8.0 1.4 copy.64
  9.4 1.1 copy.76
  10.5 0.7 fusion.71
  11.8 0.6 iota_compare_fusion
  12.5 56.9 %all-gather.5.cloned.1.call-done = bf16[4096,132]{0,1:T(8,128)(2,1)} async-done(((bf16[256,132]{0,1:T(8,128)(2,1)}), bf16[4096,132]{0,1:T(8,128)(2,1)}) %all-gather.5.cloned.1.call-update) | async-done | bytes 1081360 | tf_op jit(solution)/shard_map/all_gather | solution.py:142
  69.4 1.7 fusion.46
  71.1 0.6 fusion.68
  71.7 0.1 copy.93
  72.0 0.3 reduce_window_sum.36
  72.3 0.1 copy.68
  72.4 0.5 copy-done.11
  73.0 0.7 copy.69
  73.7 0.2 reduce_window_sum.35
  73.9 0.1 copy.66
  74.0 0.7 fusion.29
  74.6 2.6 %all-gather = bf16[136,32,64]{2,1,0:T(8,128)(2,1)S(1)} all-gather(bf16[68,32,64]{2,1,0:T(8,128)(2,1)S(1)} %fusion.29), channel_id=2, replica_groups=mesh['dp'=16,'ctx'=2] {'ctx'}, dimensions={0}, use_global_device_ids=true | all-gather | bytes 835584 | tf_op jit(solution)/shard_map/all_gather | solution.py:15
  77.3 0.2 dynamic-update-slice
  77.5 2.4 %all-reduce.4 = bf16[136]{0:T(256)(128)(2,1)S(1)} all-reduce(bf16[136]{0:T(256)(128)(2,1)S(1)} %dynamic-update-slice), channel_id=3, replica_groups=mesh['dp'=16,'ctx'=2] {'ctx'}, use_global_device_ids=true, to_apply=%add.4 | all-reduce | flops 136 | bytes 544
  80.0 0.1 reshape.510
  80.0 0.1 broadcast.329.clone
  80.2 0.3 while.20
  80.2 0.3 convert_add_fusion.4
  80.5 2.4 %fusion.13 = (f32[68,128]{1,0:T(8,128)}, bf16[128,64]{0,1:T(8,128)(2,1)}) fusion(f32[128,64]{0,1:T(8,128)} %fusion.68, f32[68,128]{1,0:T(8,128)} %copy.69, f32[68,32,64]{2,1,0:T(8,128)S(1)} %get-tuple-element.513, bf16[128,68,32]{0,2,1:T(8,128)(2,1)} %bitcast.174), kind=kOutput, calls=%fused_computation.23 | convolution fusion | flops 38419968 | bytes 1232896 | tf_op jit(solution)/shard_map/transpose(jvp())/while/body/eval_jaxpr/shp,hsn->hpn/dot_general | solution.py:58
  82.9 0.7 fusion.28
  83.6 2.7 %all-gather.2 = bf16[136,32,64]{2,1,0:T(8,128)(2,1)} all-gather(bf16[68,32,64]{2,1,0:T(8,128)(2,1)S(1)} %fusion.28), channel_id=4, replica_groups=mesh['dp'=16,'ctx'=2] {'ctx'}, dimensions={0}, use_global_device_ids=true | all-gather | bytes 835584 | tf_op jit(solution)/shard_map/all_gather | solution.py:15
  86.4 0.1 broadcast.329.clone.1
  86.5 0.2 while.21
  86.7 0.6 multiply_reduce_fusion
  87.3 0.4 copy-done.2
  87.7 1.3 fusion.27
  89.1 0.8 convolution_bitcast_fusion.2
  89.9 0.9 copy.78
  90.7 0.7 copy.73
  91.5 0.6 fusion.61
  92.1 0.6 bitcast_multiply_fusion.6
  92.7 1.5 copy.80
  94.2 1.6 copy.70
  95.7 6.0 %fusion.11 = (f32[68,128]{1,0:T(8,128)}, f32[68,128]{1,0:T(8,128)}, f32[68,128]{1,0:T(8,128)}, bf16[128,128]{1,0:T(8,128)(2,1)}) fusion(f32[68,128]{1,0:T(8,128)} %copy.73, f32[68,128]{1,0:T(8,128)} %bitcast.177, f32[128,128]{1,0:T(8,128)} %copy.70, pred[128,128]{1,0:T(8,128)(4,1)} %iota_compare_fusion, bf16[68,32,128]{2,1,0:T(8,128)(2,1)} %bitcast.164, ...), kind=kOutput, calls=%fused_computation.19 | convolution fusion | flops 90200576 | bytes 1402880 | tf_op jit(solution)/shard_map/transpose(jvp())/while/body/eval_jaxpr/hts,shp->thp/dot_general | solution.py:76
  101.7 1.5 copy.82
  103.2 1.5 copy.83
  104.7 1.6 fusion.57
  106.2 0.9 copy.84
  107.2 1.9 reduce_window_sum.37
  109.0 1.5 copy.85
  110.5 1.5 copy.79
  112.0 1.4 copy.86
  113.4 1.0 fusion.50
  114.4 1.0 fusion.41
  115.4 1.9 convolution_bitcast_fusion
  118.1 0.1 copy-done.10
  118.2 1.1 bitcast_multiply_fusion.2
  119.4 2.0 fusion.42
  121.4 1.5 fusion.44
  123.0 2.0 fusion.30
  125.0 0.5 fusion.33
  125.5 72.9 %reduce-scatter.4.cloned.1.call-done = f32[256,132]{0,1:T(8,128)} async-done(((f32[4096,132]{0,1:T(8,128)}), f32[256,132]{0,1:T(8,128)}) %reduce-scatter.4.cloned.1.call-update) | async-done | bytes 135184 | tf_op jit(solution)/shard_map/reduce_scatter | solution.py:157
  198.4 3.6 %fusion = f32[256,72]{0,1:T(8,128)S(1)} fusion(f32[256,132]{0,1:T(8,128)} %reduce-scatter.4.cloned.1.call-done), kind=kCustom, calls=%all-reduce-scatter | all-reduce-scatter fusion | flops 36865 | bytes 209408
  202.0 2.3 %collective-permute-start = (f32[256,6]{0,1:T(8,128)S(1)}, f32[256,6]{0,1:T(8,128)S(1)}, u32[]{:S(2)}, u32[]{:S(2)}) collective-permute-start(f32[256,6]{0,1:T(8,128)S(1)} %slice.28), channel_id=1, source_target_pairs={{0,1},{2,3},{4,5},{6,7},{8,9},{10,11},{12,13},{14,15},{16,17},{18,... | collective-permute-start | bytes 18440
  204.3 0.1 fusion.60
  204.4 0.7 copy.89
  205.1 1.1 copy.88
  206.2 0.1 concatenate
  206.3 0.6 dynamic-slice_multiply_fusion
  (69 shorter events, 0.6 us)
Async XLA Ops:
  7.2 62.2 %copy-start = (bf16[1,128,4096]{2,1,0:T(8,128)(2,1)S(1)}, bf16[1,128,4096]{2,1,0:T(8,128)(2,1)}, u32[]{:S(2)}) copy-start(bf16[1,128,4096]{2,1,0:T(8,128)(2,1)} %param.12) | copy-start | bytes 3145732
  7.2 2.2 %copy-start.4 = (bf16[1,128,2176]{2,1,0:T(8,128)(2,1)S(1)}, bf16[1,128,2176]{2,1,0:T(8,128)(2,1)}, u32[]{:S(2)}) copy-start(bf16[1,128,2176]{2,1,0:T(8,128)(2,1)} %param.13) | copy-start | bytes 1671172
  7.2 62.2 %all-gather.5.cloned.1.call-start = ((), (), s32[]{:S(2)}) async-start(), calls=%async_computation.1 | async-start | bytes 1183744 | tf_op jit(solution)/shard_map/all_gather | solution.py:142
  7.9 190.4 %reduce-scatter.4.cloned.1.call-start = ((), (), s32[]{:S(2)}) async-start(), calls=%async_computation.2 | async-start | bytes 2367488 | tf_op jit(solution)/shard_map/reduce_scatter | solution.py:157
  8.0 2.5 %copy-start.24 = (u32[32]{0:T(128)S(1)}, u32[32]{0:T(128)}, u32[]{:S(2)}) copy-start(u32[32]{0:T(128)} %constant.223) | copy-start | bytes 388
  8.0 4.4 %copy-start.26 = (f32[68]{0:T(128)S(1)}, f32[68]{0:T(128)}, u32[]{:S(2)}) copy-start(f32[68]{0:T(128)} %param.16) | copy-start | bytes 820
  8.0 4.4 %copy-start.7 = (bf16[1,128,64]{1,2,0:T(8,128)(2,1)S(1)}, bf16[1,128,64]{1,2,0:T(8,128)(2,1)}, u32[]{:S(2)}) copy-start(bf16[1,128,64]{1,2,0:T(8,128)(2,1)} %param.14) | copy-start | bytes 49156
  9.4 64.6 %copy-start.1 = (bf16[1,128,2176]{1,2,0:T(8,128)(2,1)}, bf16[1,128,2176]{1,2,0:T(8,128)(2,1)S(1)}, u32[]{:S(2)}) copy-start(bf16[1,128,2176]{1,2,0:T(8,128)(2,1)S(1)} %copy.64) | copy-start | bytes 1671172
  12.4 59.4 %copy-start.23 = (f32[68]{0:T(128)}, f32[68]{0:T(128)S(1)}, u32[]{:S(2)}) copy-start(f32[68]{0:T(128)S(1)} %exponential_negate_fusion) | copy-start | bytes 820
  12.4 59.4 %copy-start.22 = (f32[68]{0:T(128)S(1)}, f32[68]{0:T(128)}, u32[]{:S(2)}) copy-start(f32[68]{0:T(128)} %param.17) | copy-start | bytes 820
  71.1 18.0 %copy-start.6 = (f32[128,132]{0,1:T(8,128)}, f32[128,132]{0,1:T(8,128)S(1)}, u32[]{:S(2)}) copy-start(f32[128,132]{0,1:T(8,128)S(1)} %fusion.46) | copy-start | bytes 202756
  72.3 0.6 copy-start.11
  72.9 18.6 %copy-start.21 = (f32[68]{0:T(128)}, f32[68]{0:T(128)S(1)}, u32[]{:S(2)}) copy-start(f32[68]{0:T(128)S(1)} %slice_bitcast_fusion) | copy-start | bytes 820
  80.5 2.4 %copy-start.5 = (bf16[1,128,2176]{1,2,0:T(8,128)(2,1)S(1)}, bf16[1,128,2176]{1,2,0:T(8,128)(2,1)}, u32[]{:S(2)}) copy-start(bf16[1,128,2176]{1,2,0:T(8,128)(2,1)} %copy.76) | copy-start | bytes 1671172
  80.5 2.4 %copy-start.13 = (f32[68,128]{1,0:T(8,128)S(1)}, f32[68,128]{1,0:T(8,128)}, u32[]{:S(2)}) copy-start(f32[68,128]{1,0:T(8,128)} %copy.69) | copy-start | bytes 104452
  80.5 2.4 %copy-start.15 = (f32[128,64]{0,1:T(8,128)S(1)}, f32[128,64]{0,1:T(8,128)}, u32[]{:S(2)}) copy-start(f32[128,64]{0,1:T(8,128)} %fusion.68) | copy-start | bytes 98308
  86.7 1.1 copy-start.2
  86.7 1.0 copy-start.8
  101.7 12.7 %copy-start.9 = (bf16[1,128,64]{1,2,0:T(8,128)(2,1)S(1)}, bf16[1,128,64]{1,2,0:T(8,128)(2,1)}, u32[]{:S(2)}) copy-start(bf16[1,128,64]{1,2,0:T(8,128)(2,1)} %param.14) | copy-start | bytes 49156
  117.3 0.8 copy-start.10
  119.4 2.0 copy-start.17
  119.4 3.6 %copy-start.3 = (bf16[1,128,2176]{1,2,0:T(8,128)(2,1)S(1)}, bf16[1,128,2176]{1,2,0:T(8,128)(2,1)}, u32[]{:S(2)}) copy-start(bf16[1,128,2176]{1,2,0:T(8,128)(2,1)} %copy-done.1) | copy-start | bytes 1671172
  119.4 3.5 %copy-start.12 = (f32[1,68,128]{2,1,0:T(8,128)S(1)}, f32[1,68,128]{2,1,0:T(8,128)}, u32[]{:S(2)}) copy-start(f32[1,68,128]{2,1,0:T(8,128)} %copy-done.11) | copy-start | bytes 104452
  119.4 3.5 %copy-start.18 = (f32[128,128]{1,0:T(8,128)S(1)}, f32[128,128]{1,0:T(8,128)}, u32[]{:S(2)}) copy-start(f32[128,128]{1,0:T(8,128)} %copy.70) | copy-start | bytes 196612
  119.4 3.5 %copy-start.19 = (f32[68,128]{1,0:T(8,128)S(1)}, f32[68,128]{1,0:T(8,128)}, u32[]{:S(2)}) copy-start(f32[68,128]{1,0:T(8,128)} %copy.73) | copy-start | bytes 104452
  119.4 3.5 %copy-start.20 = (pred[128,128]{1,0:T(8,128)(4,1)S(1)}, pred[128,128]{1,0:T(8,128)(4,1)}, u32[]{:S(2)}) copy-start(pred[128,128]{1,0:T(8,128)(4,1)} %iota_compare_fusion) | copy-start | bytes 49156
  123.0 2.0 copy-start.14
  123.0 2.0 copy-start.16
  123.0 2.0 copy-start.25
  202.0 4.1 %collective-permute-start = (f32[256,6]{0,1:T(8,128)S(1)}, f32[256,6]{0,1:T(8,128)S(1)}, u32[]{:S(2)}, u32[]{:S(2)}) collective-permute-start(f32[256,6]{0,1:T(8,128)S(1)} %slice.28), channel_id=1, source_target_pairs={{0,1},{2,3},{4,5},{6,7},{8,9},{10,11},{12,13},{14,15},{16,17},{18,... | collective-permute-start | bytes 18440
Sparse Core Ops, SparseCore 0:
  10.7 58.5 all-gather.4
  117.5 80.8 reduce-scatter.3
where the time goes:
time: 215 us; the launch traced here: 214 us
  waiting for transfers between devices  130 us (60%)
  matrix products  22.4 us (10%)
  local copies, waits for them, and re-layouts  20.8 us (10%)
  between operations  15.9 us (7%)
  blocking collectives  11.4 us (5%)
  other arithmetic  10.2 us (5%)
  starting transfers between devices  2.33 us (1%)
    reduce_scatter x1, waiting for transfers between devices, per_device(): lax.psum_scatter(lax.dot_general(tokens, proj_grad, contract, preferred_e...  72.9 us
    all_gather x1, waiting for transfers between devices, per_device(): w_full = lax.all_gather(w_in, 'dp', axis=0, tiled=True)  56.9 us
    dot_general x2, matrix products, block_advance(): jnp.einsum('hts,shp->thp', mixing, inner_c, preferred_element_type=jnp.fl...  7.92 us
    unnamed x64, local copies, waits for them, and re-layouts  6.5 us
    unnamed x2, blocking collectives  6.08 us
    all_gather x2, blocking collectives, entering(): lax.all_gather(a.astype(kind), axis)  5.35 us
  transfers between devices with their start and end apart: 3, of which 2 were waited for; matrix products, arithmetic and copies ran while one was open for 6% of the time, Pallas kernels for 0%

commit v1 on v0

--- a/solution.py
+++ b/solution.py
@@ -139,7 +139,15 @@
     inner_rows = inner_act[0]
     c_rows = readout[0]
     grad_rows = grad_out[0]
-    w_full = lax.all_gather(w_in, "dp", axis=0, tiled=True)
+    ways, here = (lax.axis_size("dp"), lax.axis_index("dp"))
+    grown, reach = (w_in, 1)
+    while reach < ways:
+        theirs = lax.ppermute(grown, "dp", [(d, d ^ reach) for d in range(ways)])
+        mine_first = jnp.concatenate([grown, theirs], axis=0)
+        theirs_first = jnp.concatenate([theirs, grown], axis=0)
+        grown = jnp.where(here & reach == 0, mine_first, theirs_first)
+        reach = 2 * reach
+    w_full = grown
     projected = jnp.dot(tokens, w_full, preferred_element_type=jnp.float32)
     decay_total, own_state = local_summary(projected, inner_rows, a_log, dt_bias)
     entry_part = entry_weights(projected, c_rows, grad_rows, a_log, dt_bias)

time: 215 us -> 201 us (0.935)
  waiting for transfers between devices: 130 us -> 100 us
  starting transfers between devices: 2.33 us -> 13.5 us
  other arithmetic: 10.2 us -> 14.8 us
    all_gather x1 -> x0, waiting for transfers between devices: 56.9 us -> none  [per_device(): w_full = lax.all_gather(w_in, 'dp', axis=0, tiled=True)]
    ppermute x0 -> x4, waiting for transfers between devices: none -> 26.3 us  [per_device(): theirs = lax.ppermute(grown, 'dp', [(d, d ^ reach) for d in range(ways)])]
    ppermute x0 -> x4, starting transfers between devices: none -> 11.2 us  [per_device(): theirs = lax.ppermute(grown, 'dp', [(d, d ^ reach) for d in range(ways)])]
    unnamed x64 -> x65, local copies, waits for them, and re-layouts: 6.5 us -> 5.34 us
  transfers between devices with their start and end apart: 3 -> 6, of which waited for: 2 -> 5; matrix products, arithmetic and copies ran while one was open for 6% -> 6% of each run, Pallas kernels for 0% -> 0%
where the time goes in v1:
time: 201 us; the launch traced here: 200 us
  waiting for transfers between devices  100 us (50%)
  local copies, waits for them, and re-layouts  21.7 us (11%)
  matrix products  21.4 us (11%)
  between operations  15.9 us (8%)
  other arithmetic  14.8 us (7%)
  starting transfers between devices  13.5 us (7%)
  blocking collectives  12.1 us (6%)
    reduce_scatter x1, waiting for transfers between devices, per_device(): lax.psum_scatter(lax.dot_general(tokens, proj_grad, contract, preferred_e...  74 us
    ppermute x4, waiting for transfers between devices, per_device(): theirs = lax.ppermute(grown, 'dp', [(d, d ^ reach) for d in range(ways)])  26.3 us
    ppermute x4, starting transfers between devices, per_device(): theirs = lax.ppermute(grown, 'dp', [(d, d ^ reach) for d in range(ways)])  11.2 us
    dot_general x2, matrix products, block_advance(): jnp.einsum('hts,shp->thp', mixing, inner_c, preferred_element_type=jnp.fl...  7.93 us
    unnamed x2, blocking collectives  6.08 us
    all_gather x2, blocking collectives, entering(): lax.all_gather(a.astype(kind), axis)  6.05 us
    unnamed x65, local copies, waits for them, and re-layouts  5.34 us
  transfers between devices with their start and end apart: 6, of which 5 were waited for; matrix products, arithmetic and copies ran while one was open for 6% of the time, Pallas kernels for 0%

profile of v1, /device:TPU:0, one launch (start us, length us, event | category | flops | bytes accessed | tf_op | source)
XLA Modules:
  0.0 200.1 jit_solution(46188397820309187)
XLA Ops:
  7.2 3.0 %collective-permute-start = (bf16[256,132]{0,1:T(8,128)(2,1)}, bf16[256,132]{0,1:T(8,128)(2,1)S(1)}, u32[]{:S(2)}, u32[]{:S(2)}) collective-permute-start(bf16[256,132]{0,1:T(8,128)(2,1)} %param.15), channel_id=1, source_target_pairs={{0,2},{2,0},{4,6},{6,4},{8,10},{10,8},{12,14},{14,12},{16,18},{18,... | collective-permute-start | bytes 202760 | tf_op jit(solution)/shard_map/ppermute | solution.py:145
  10.2 2.5 %collective-permute-done = bf16[256,132]{0,1:T(8,128)(2,1)S(1)} collective-permute-done((bf16[256,132]{0,1:T(8,128)(2,1)}, bf16[256,132]{0,1:T(8,128)(2,1)S(1)}, u32[]{:S(2)}, u32[]{:S(2)}) %collective-permute-start) | collective-permute-done | bytes 67616 | tf_op jit(solution)/shard_map/ppermute | solution.py:145
  12.7 1.0 maximum_select_fusion.4
  13.7 2.1 %collective-permute-start.1 = (bf16[512,132]{0,1:T(8,128)(2,1)S(1)}, bf16[512,132]{0,1:T(8,128)(2,1)S(1)}, u32[]{:S(2)}, u32[]{:S(2)}) collective-permute-start(bf16[512,132]{0,1:T(8,128)(2,1)S(1)} %maximum_select_fusion.4), channel_id=1, source_target_pairs={{0,4},{2,6},{4,0},{6,2},{8,12},{10,14},{12,8},{14,10},{16,20},{18,... | collective-permute-start | bytes 405512 | tf_op jit(solution)/shard_map/ppermute | solution.py:145
  15.9 3.0 %collective-permute-done.1 = bf16[512,132]{0,1:T(8,128)(2,1)S(1)} collective-permute-done((bf16[512,132]{0,1:T(8,128)(2,1)S(1)}, bf16[512,132]{0,1:T(8,128)(2,1)S(1)}, u32[]{:S(2)}, u32[]{:S(2)}) %collective-permute-start.1) | collective-permute-done | bytes 135200 | tf_op jit(solution)/shard_map/ppermute | solution.py:145
  19.0 2.1 %collective-permute-start.2 = (bf16[1024,132]{0,1:T(8,128)(2,1)S(1)}, bf16[1024,132]{0,1:T(8,128)(2,1)S(1)}, u32[]{:S(2)}, u32[]{:S(2)}) collective-permute-start(bf16[1024,132]{0,1:T(8,128)(2,1)S(1)} %maximum_select_fusion.3), channel_id=1, source_target_pairs={{0,8},{2,10},{4,12},{6,14},{8,0},{10,2},{12,4},{14,6},{16,24},{18,... | collective-permute-start | bytes 811016 | tf_op jit(solution)/shard_map/ppermute | solution.py:145
  21.1 0.3 copy.78
  21.5 1.0 copy.65
  22.5 0.7 fusion.76
  23.9 1.8 collective-permute-done.2
  25.8 4.0 %collective-permute-start.3 = (bf16[2048,132]{0,1:T(8,128)(2,1)S(1)}, bf16[2048,132]{0,1:T(8,128)(2,1)S(1)}, u32[]{:S(2)}, u32[]{:S(2)}) collective-permute-start(bf16[2048,132]{0,1:T(8,128)(2,1)S(1)} %maximum_select_fusion.2), channel_id=1, source_target_pairs={{0,16},{2,18},{4,20},{6,22},{8,24},{10,26},{12,28},{14,30},{16,0},... | collective-permute-start | bytes 1622024 | tf_op jit(solution)/shard_map/ppermute | solution.py:145
  29.8 0.6 iota_compare_fusion
  30.4 0.6 bitcast_convert_fusion.2
  31.0 19.0 %collective-permute-done.3 = bf16[2048,132]{0,1:T(8,128)(2,1)S(1)} collective-permute-done((bf16[2048,132]{0,1:T(8,128)(2,1)S(1)}, bf16[2048,132]{0,1:T(8,128)(2,1)S(1)}, u32[]{:S(2)}, u32[]{:S(2)}) %collective-permute-start.3) | collective-permute-done | bytes 540704 | tf_op jit(solution)/shard_map/ppermute | solution.py:145
  50.0 0.5 convolution_bitcast_fusion.2
  50.6 0.8 fusion.75
  51.4 0.3 reduce_window_sum.36
  51.8 0.5 copy-done.10
  52.6 0.7 fusion.28
  53.3 2.6 %all-gather.2 = bf16[136,32,64]{2,1,0:T(8,128)(2,1)S(1)} all-gather(bf16[68,32,64]{2,1,0:T(8,128)(2,1)S(1)} %fusion.28), channel_id=4, replica_groups=mesh['dp'=16,'ctx'=2] {'ctx'}, dimensions={0}, use_global_device_ids=true | all-gather | bytes 835584 | tf_op jit(solution)/shard_map/all_gather | solution.py:15
  56.0 0.2 dynamic-update-slice
  56.2 2.4 %all-reduce.4 = bf16[136]{0:T(256)(128)(2,1)S(1)} all-reduce(bf16[136]{0:T(256)(128)(2,1)S(1)} %dynamic-update-slice), channel_id=3, replica_groups=mesh['dp'=16,'ctx'=2] {'ctx'}, use_global_device_ids=true, to_apply=%add.4 | all-reduce | flops 136 | bytes 544
  58.6 0.6 reshape.510
  59.4 0.2 reduce_window_sum.35
  59.7 1.8 fusion.29
  61.5 3.4 %all-gather = bf16[136,32,64]{2,1,0:T(8,128)(2,1)} all-gather(bf16[68,32,64]{2,1,0:T(8,128)(2,1)S(1)} %fusion.29), channel_id=2, replica_groups=mesh['dp'=16,'ctx'=2] {'ctx'}, dimensions={0}, use_global_device_ids=true | all-gather | bytes 835584 | tf_op jit(solution)/shard_map/all_gather | solution.py:15
  65.1 1.5 while.20
  65.1 1.3 convert_add_fusion.4
  66.6 2.3 %fusion.13 = (f32[68,128]{1,0:T(8,128)}, bf16[128,64]{0,1:T(8,128)(2,1)}) fusion(f32[128,64]{0,1:T(8,128)} %copy-done.15, f32[68,128]{1,0:T(8,128)S(1)} %copy-done.13, f32[68,32,64]{2,1,0:T(8,128)S(1)} %get-tuple-element.513, bf16[128,68,32]{0,2,1:T(8,128)(2,1)} %bitcast.178), kind=kOutput, calls=%fused_computation.23 | convolution fusion | flops 38419968 | bytes 1232896 | tf_op jit(solution)/shard_map/transpose(jvp())/while/body/eval_jaxpr/shp,hsn->hpn/dot_general | solution.py:58
  68.9 0.6 multiply_reduce_fusion
  69.5 0.5 copy-done.1
  70.0 1.3 fusion.27
  71.3 0.7 convolution_bitcast_fusion.3
  72.1 0.6 bitcast_multiply_fusion.6
  72.7 0.9 copy.80
  73.5 1.3 fusion.65
  74.8 1.5 copy.82
  76.3 1.5 copy.75
  77.9 1.6 copy.72
  79.5 6.0 %fusion.11 = (f32[68,128]{1,0:T(8,128)}, f32[68,128]{1,0:T(8,128)}, f32[68,128]{1,0:T(8,128)}, bf16[128,128]{1,0:T(8,128)(2,1)}) fusion(f32[68,128]{1,0:T(8,128)} %copy.75, f32[68,128]{1,0:T(8,128)} %bitcast.180, f32[128,128]{1,0:T(8,128)} %copy.72, pred[128,128]{1,0:T(8,128)(4,1)} %iota_compare_fusion, bf16[68,32,128]{2,1,0:T(8,128)(2,1)} %bitcast.167, ...), kind=kOutput, calls=%fused_computation.19 | convolution fusion | flops 90200576 | bytes 1402880 | tf_op jit(solution)/shard_map/transpose(jvp())/while/body/eval_jaxpr/hts,shp->thp/dot_general | solution.py:76
  85.4 1.5 copy.84
  86.9 1.5 copy.85
  88.4 1.7 fusion.62
  90.1 1.5 copy.86
  91.6 2.6 %reduce_window_sum.37 = f32[1,68,128]{2,1,0:T(8,128)} reduce-window(f32[1,68,128]{2,1,0:T(8,128)} %copy.86, f32[]{:T(128)} %constant.209.clone.1), window={size=1x1x128 pad=0_0x0_0x0_127}, to_apply=%region_15.16 | reduce-window | flops 1105408 | bytes 69636 | tf_op jit(solution)/shard_map/transpose(jvp(jit(cumsum)))/reduce_window_sum | solution.py:51
  94.2 1.5 copy.87
  95.7 1.5 copy.81
  97.2 1.4 copy.88
  98.6 1.0 fusion.55
  99.6 1.0 fusion.47
  100.6 1.9 convolution_bitcast_fusion
  103.4 0.7 copy.77
  104.1 1.1 bitcast_multiply_fusion.2
  105.3 2.0 fusion.48
  107.3 0.8 fusion.50
  108.2 2.0 fusion.30
  110.2 0.5 fusion.33
  110.7 74.0 %reduce-scatter.4.cloned.1.call-done = f32[256,132]{0,1:T(8,128)} async-done(((f32[4096,132]{0,1:T(8,128)}), f32[256,132]{0,1:T(8,128)}) %reduce-scatter.4.cloned.1.call-update) | async-done | bytes 135184 | tf_op jit(solution)/shard_map/reduce_scatter | solution.py:165
  184.7 3.6 %fusion = f32[256,72]{0,1:T(8,128)S(1)} fusion(f32[256,132]{0,1:T(8,128)} %reduce-scatter.4.cloned.1.call-done), kind=kCustom, calls=%all-reduce-scatter | all-reduce-scatter fusion | flops 36865 | bytes 209408
  188.3 2.3 %collective-permute-start.4 = (f32[256,6]{0,1:T(8,128)S(1)}, f32[256,6]{0,1:T(8,128)S(1)}, u32[]{:S(2)}, u32[]{:S(2)}) collective-permute-start(f32[256,6]{0,1:T(8,128)S(1)} %slice.28), channel_id=1, source_target_pairs={{0,1},{2,3},{4,5},{6,7},{8,9},{10,11},{12,13},{14,15},{16,17},{18,... | collective-permute-start | bytes 18440
  190.7 0.7 copy.91
  191.4 1.1 copy.90
  192.5 0.1 concatenate.32
  192.6 0.6 dynamic-slice_multiply_fusion
  (78 shorter events, 1.5 us)
Async XLA Ops:
  7.2 42.9 %copy-start = (bf16[1,128,4096]{2,1,0:T(8,128)(2,1)S(1)}, bf16[1,128,4096]{2,1,0:T(8,128)(2,1)}, u32[]{:S(2)}) copy-start(bf16[1,128,4096]{2,1,0:T(8,128)(2,1)} %param.12) | copy-start | bytes 3145732
  7.2 14.0 %copy-start.5 = (bf16[1,128,2176]{2,1,0:T(8,128)(2,1)S(1)}, bf16[1,128,2176]{2,1,0:T(8,128)(2,1)}, u32[]{:S(2)}) copy-start(bf16[1,128,2176]{2,1,0:T(8,128)(2,1)} %param.13) | copy-start | bytes 1671172
  7.2 14.3 %copy-start.6 = (bf16[1,128,2176]{2,1,0:T(8,128)(2,1)S(1)}, bf16[1,128,2176]{2,1,0:T(8,128)(2,1)}, u32[]{:S(2)}) copy-start(bf16[1,128,2176]{2,1,0:T(8,128)(2,1)} %param.19) | copy-start | bytes 1671172
  7.2 177.5 %reduce-scatter.4.cloned.1.call-start = ((), (), s32[]{:S(2)}) async-start(), calls=%async_computation.1 | async-start | bytes 2367488 | tf_op jit(solution)/shard_map/reduce_scatter | solution.py:165
  7.2 5.5 %collective-permute-start = (bf16[256,132]{0,1:T(8,128)(2,1)}, bf16[256,132]{0,1:T(8,128)(2,1)S(1)}, u32[]{:S(2)}, u32[]{:S(2)}) collective-permute-start(bf16[256,132]{0,1:T(8,128)(2,1)} %param.15), channel_id=1, source_target_pairs={{0,2},{2,0},{4,6},{6,4},{8,10},{10,8},{12,14},{14,12},{16,18},{18,... | collective-permute-start | bytes 202760 | tf_op jit(solution)/shard_map/ppermute | solution.py:145
  13.7 5.2 %collective-permute-start.1 = (bf16[512,132]{0,1:T(8,128)(2,1)S(1)}, bf16[512,132]{0,1:T(8,128)(2,1)S(1)}, u32[]{:S(2)}, u32[]{:S(2)}) collective-permute-start(bf16[512,132]{0,1:T(8,128)(2,1)S(1)} %maximum_select_fusion.4), channel_id=1, source_target_pairs={{0,4},{2,6},{4,0},{6,2},{8,12},{10,14},{12,8},{14,10},{16,20},{18,... | collective-permute-start | bytes 405512 | tf_op jit(solution)/shard_map/ppermute | solution.py:145
  19.0 6.7 %collective-permute-start.2 = (bf16[1024,132]{0,1:T(8,128)(2,1)S(1)}, bf16[1024,132]{0,1:T(8,128)(2,1)S(1)}, u32[]{:S(2)}, u32[]{:S(2)}) collective-permute-start(bf16[1024,132]{0,1:T(8,128)(2,1)S(1)} %maximum_select_fusion.3), channel_id=1, source_target_pairs={{0,8},{2,10},{4,12},{6,14},{8,0},{10,2},{12,4},{14,6},{16,24},{18,... | collective-permute-start | bytes 811016 | tf_op jit(solution)/shard_map/ppermute | solution.py:145
  21.1 1.4 copy-start.24
  21.4 31.2 %copy-start.7 = (bf16[1,128,2176]{1,2,0:T(8,128)(2,1)}, bf16[1,128,2176]{1,2,0:T(8,128)(2,1)S(1)}, u32[]{:S(2)}) copy-start(bf16[1,128,2176]{1,2,0:T(8,128)(2,1)S(1)} %copy.78) | copy-start | bytes 1671172
  21.5 8.9 %copy-start.26 = (f32[68]{0:T(128)S(1)}, f32[68]{0:T(128)}, u32[]{:S(2)}) copy-start(f32[68]{0:T(128)} %param.16) | copy-start | bytes 820
  21.5 8.9 %copy-start.8 = (bf16[1,128,64]{1,2,0:T(8,128)(2,1)S(1)}, bf16[1,128,64]{1,2,0:T(8,128)(2,1)}, u32[]{:S(2)}) copy-start(bf16[1,128,64]{1,2,0:T(8,128)(2,1)} %param.14) | copy-start | bytes 49156
  25.8 24.2 %collective-permute-start.3 = (bf16[2048,132]{0,1:T(8,128)(2,1)S(1)}, bf16[2048,132]{0,1:T(8,128)(2,1)S(1)}, u32[]{:S(2)}, u32[]{:S(2)}) collective-permute-start(bf16[2048,132]{0,1:T(8,128)(2,1)S(1)} %maximum_select_fusion.2), channel_id=1, source_target_pairs={{0,16},{2,18},{4,20},{6,22},{8,24},{10,26},{12,28},{14,30},{16,0},... | collective-permute-start | bytes 1622024 | tf_op jit(solution)/shard_map/ppermute | solution.py:145
  30.4 20.2 %copy-start.23 = (f32[68]{0:T(128)}, f32[68]{0:T(128)S(1)}, u32[]{:S(2)}) copy-start(f32[68]{0:T(128)S(1)} %exponential_negate_fusion) | copy-start | bytes 820
  31.0 19.5 %copy-start.21 = (f32[68]{0:T(128)S(1)}, f32[68]{0:T(128)}, u32[]{:S(2)}) copy-start(f32[68]{0:T(128)} %param.17) | copy-start | bytes 820
  51.7 0.6 copy-start.10
  51.8 0.8 copy-start.22
  52.5 3.4 %copy-start.12 = (f32[68,128]{1,0:T(8,128)}, f32[68,128]{1,0:T(8,128)S(1)}, u32[]{:S(2)}) copy-start(f32[68,128]{1,0:T(8,128)S(1)} %copy.71) | copy-start | bytes 104452
  52.6 3.3 %copy-start.15 = (f32[128,64]{0,1:T(8,128)}, f32[128,64]{0,1:T(8,128)S(1)}, u32[]{:S(2)}) copy-start(f32[128,64]{0,1:T(8,128)S(1)} %copy.68) | copy-start | bytes 98308
  61.4 3.6 %copy-start.27 = (bf16[2,68]{1,0:T(2,128)(2,1)S(1)}, bf16[2,68]{1,0:T(2,128)(2,1)}, u32[]{:S(2)}) copy-start(bf16[2,68]{1,0:T(2,128)(2,1)} %get-tuple-element.694) | copy-start | bytes 820
  65.0 1.6 copy-start.13
  68.9 1.1 copy-start.1
  99.6 1.0 copy-start.3
  102.6 0.8 copy-start.9
  105.3 2.0 %copy-start.17 = (bf16[128,128]{1,0:T(8,128)(2,1)S(1)}, bf16[128,128]{1,0:T(8,128)(2,1)}, u32[]{:S(2)}) copy-start(bf16[128,128]{1,0:T(8,128)(2,1)} %get-tuple-element.538) | copy-start | bytes 98308
  105.3 2.9 %copy-start.2 = (bf16[1,128,2176]{1,2,0:T(8,128)(2,1)S(1)}, bf16[1,128,2176]{1,2,0:T(8,128)(2,1)}, u32[]{:S(2)}) copy-start(bf16[1,128,2176]{1,2,0:T(8,128)(2,1)} %copy.65) | copy-start | bytes 1671172
  105.3 2.8 %copy-start.11 = (f32[1,68,128]{2,1,0:T(8,128)S(1)}, f32[1,68,128]{2,1,0:T(8,128)}, u32[]{:S(2)}) copy-start(f32[1,68,128]{2,1,0:T(8,128)} %copy-done.10) | copy-start | bytes 104452
  105.3 2.8 %copy-start.18 = (f32[128,128]{1,0:T(8,128)S(1)}, f32[128,128]{1,0:T(8,128)}, u32[]{:S(2)}) copy-start(f32[128,128]{1,0:T(8,128)} %copy.72) | copy-start | bytes 196612
  105.3 2.8 %copy-start.19 = (f32[68,128]{1,0:T(8,128)S(1)}, f32[68,128]{1,0:T(8,128)}, u32[]{:S(2)}) copy-start(f32[68,128]{1,0:T(8,128)} %copy.75) | copy-start | bytes 104452
  105.3 2.8 %copy-start.20 = (pred[128,128]{1,0:T(8,128)(4,1)S(1)}, pred[128,128]{1,0:T(8,128)(4,1)}, u32[]{:S(2)}) copy-start(pred[128,128]{1,0:T(8,128)(4,1)} %iota_compare_fusion) | copy-start | bytes 49156
  108.1 2.0 %copy-start.14 = (f32[68,128]{1,0:T(8,128)S(1)}, f32[68,128]{1,0:T(8,128)}, u32[]{:S(2)}) copy-start(f32[68,128]{1,0:T(8,128)} %copy-done.12) | copy-start | bytes 104452
  108.2 2.0 %copy-start.16 = (f32[128,64]{0,1:T(8,128)S(1)}, f32[128,64]{0,1:T(8,128)}, u32[]{:S(2)}) copy-start(f32[128,64]{0,1:T(8,128)} %copy-done.15) | copy-start | bytes 98308
  108.2 2.0 %copy-start.25 = (f32[68]{0:T(128)S(1)}, f32[68]{0:T(128)}, u32[]{:S(2)}) copy-start(f32[68]{0:T(128)} %param.18) | copy-start | bytes 820
  110.2 80.4 %copy-start.4 = (f32[128,68]{1,0:T(8,128)S(1)}, f32[128,68]{1,0:T(8,128)}, u32[]{:S(2)}) copy-start(f32[128,68]{1,0:T(8,128)} %copy-done.3) | copy-start | bytes 104452
  188.3 4.2 %collective-permute-start.4 = (f32[256,6]{0,1:T(8,128)S(1)}, f32[256,6]{0,1:T(8,128)S(1)}, u32[]{:S(2)}, u32[]{:S(2)}) collective-permute-start(f32[256,6]{0,1:T(8,128)S(1)} %slice.28), channel_id=1, source_target_pairs={{0,1},{2,3},{4,5},{6,7},{8,9},{10,11},{12,13},{14,15},{16,17},{18,... | collective-permute-start | bytes 18440
Sparse Core Ops, SparseCore 0:
  102.7 81.8 reduce-scatter.3
